TPU v7x, 32 devices: a whole 2x2x4 slice. The times are simulated.
32 devices in a mesh: groups: 2 (over y), cand: 4 (over z), tgt: 2 (over x), mix: 2 (over core).
Axes of the slice: x: 2, y: 2, z: 4, core: 2. Of those that a mesh axis runs over, the one named last changes fastest.
Arguments:
- candidates: bfloat16 [8192, 1024], P(('groups', 'cand')), parts along dimension 0, may hold values from -6 to 6
- targets: bfloat16 [4096, 1024], P(('groups', 'tgt')), parts along dimension 0, may hold values from -6 to 6
- member: int32 [4096], P('groups'), parts along dimension 0, may hold values from 0 to 15
- mix_weight: float32 [64, 32], P('mix', 'groups'), parts along dimension 1, may hold values from 0.1 to 10
Outputs:
- cand_potential: float32 [64, 8192], P('mix', ('groups', 'cand')), parts along dimension 1
- tgt_potential: float32 [64, 4096], P('mix', ('groups', 'tgt')), parts along dimension 1
There are 2 independent parts, one for each index of `groups`. A program takes and returns all parts, laid end to end along the dimension named above; each array names one. Nothing has to cross between parts.
All inputs are finite; a program needn't handle non-finite values.
Results may differ from a plain program's by a relative error of at most 0.0023.
Values sent between devices are 32-bit elements; how exact they have to be, the bound alone decides.
A program may use at most 64 MiB of HBM per device.

v0:
```python
import math

import jax
import jax.numpy as jnp
from jax import lax
from jax.sharding import PartitionSpec as P

ITERS = 2


EPS_FIRST = 0.05
EPS_SECOND = 0.025


def unit_rows(embedding):
    values = embedding.astype(jnp.float32)
    mean_sq = jnp.mean(values * values, axis=1, keepdims=True)
    return (values * lax.rsqrt(mean_sq + 1e-06) * (1.0 / math.sqrt(values.shape[1]))).astype(
        jnp.bfloat16
    )


def contract_last(left, right):
    return lax.dot_general(
        left, right, (((1,), (1,)), ((), ())), preferred_element_type=jnp.float32
    )


def target_mass(own_member, member, mix_weight, cand_total):
    task_ids = jnp.arange(mix_weight.shape[1], dtype=jnp.int32)
    counts = jnp.sum((member[None, :] == task_ids[:, None]).astype(jnp.float32), axis=1)
    weight_total = jnp.dot(mix_weight, counts, precision=lax.Precision.HIGHEST)
    onehot = (own_member[None, :] == task_ids[:, None]).astype(jnp.float32)
    per_target = jnp.dot(mix_weight, onehot, precision=lax.Precision.HIGHEST)
    return per_target * (cand_total / weight_total)[:, None]


def local(candidates, targets, member, mix_weight):
    cand_rows = candidates.shape[0]
    tgt_rows = targets.shape[0]
    tgt_total = tgt_rows * lax.axis_size("tgt")
    cand_total = cand_rows * lax.axis_size("cand")
    tgt_unit = unit_rows(targets)
    scores = contract_last(unit_rows(candidates), tgt_unit)
    own_member = lax.dynamic_slice_in_dim(member, lax.axis_index("tgt") * tgt_rows, tgt_rows, 0)
    mass = target_mass(own_member, member, mix_weight, float(cand_total))
    kernel_one = jnp.exp(scores / EPS_FIRST) / tgt_total
    kernel_two = jnp.exp(scores / EPS_SECOND) / tgt_total
    scale_tgt = jnp.ones((mix_weight.shape[0], tgt_rows), jnp.float32)
    scale_cand = jnp.ones((mix_weight.shape[0], cand_rows), jnp.float32)
    for section_index, kernel in enumerate((kernel_one, kernel_two)):
        if section_index == 1:
            scale_tgt = scale_tgt * scale_tgt
        for repeat in range(ITERS):
            partial_value = lax.dot_general(
                scale_tgt, kernel, (((1,), (1,)), ((), ())), precision=lax.Precision.HIGHEST
            )
            scale_cand = 1.0 / lax.psum(partial_value, "tgt")
            column_part = jnp.dot(scale_cand, kernel, precision=lax.Precision.HIGHEST)
            share_cols = tgt_rows // lax.axis_size("cand")
            summed = lax.psum_scatter(column_part, "cand", scatter_dimension=1, tiled=True)
            own_mass = lax.dynamic_slice_in_dim(
                mass, lax.axis_index("cand") * share_cols, share_cols, 1
            )
            scale_tgt = lax.all_gather(own_mass / summed, "cand", axis=1, tiled=True)
    return (jnp.log(scale_cand), jnp.log(scale_tgt))


def solution(mesh):
    in_specs = (
        P(("groups", "cand"), None),
        P(("groups", "tgt"), None),
        P("groups"),
        P("mix", "groups"),
    )
    out_specs = (P("mix", ("groups", "cand")), P("mix", ("groups", "tgt")))
    return jax.shard_map(local, mesh=mesh, in_specs=in_specs, out_specs=out_specs, check_vma=False)
```

profile of v0, /device:TPU:0, one launch (start us, length us, event | category | flops | bytes accessed | tf_op | source)
XLA Modules:
  0.0 290.6 jit_solution(8294371134683162558)
XLA Ops:
  7.2 0.0 copy-start
  7.2 0.0 copy-start.2
  7.2 0.0 all-reduce.5.cloned.1.call-start
  7.2 0.0 copy-start.3
  7.2 2.2 fusion
  9.5 2.1 fusion.3
  11.6 0.0 copy-done.2
  11.6 0.0 copy-done.3
  11.6 2.5 fusion.6
  14.1 0.0 copy-start.1
  14.1 1.9 copy-done.1
  16.0 0.0 copy-start.5
  16.0 4.6 %fusion.15 = f32[32,1024]{1,0:T(8,128)} fusion(f32[1024,1024]{1,0:T(8,128)S(1)} %fusion.6), kind=kOutput, calls=%fused_computation.19 | convolution fusion | flops 404750336 | bytes 4325376 | tf_op jit(solution)/shard_map/dot_general | solution.py:55
  20.7 0.0 all-reduce.5.cloned.1.call-update
  20.7 0.0 reduce-scatter.5.cloned.1.call-start
  20.8 0.0 copy-done.5
  20.8 0.1 convert_reduce_fusion
  20.9 24.1 %all-reduce.5.cloned.1.call-done = f32[32,1024]{1,0:T(8,128)} async-done(((f32[32,1024]{1,0:T(8,128)}), f32[32,1024]{1,0:T(8,128)}) %all-reduce.5.cloned.1.call-update) | async-done | bytes 131088 | tf_op jit(solution)/shard_map/psum | solution.py:58
  45.0 5.9 %fusion.14 = f32[32,1024]{1,0:T(8,128)} fusion(f32[1024,1024]{1,0:T(8,128)} %copy-done.1, f32[32,1024]{1,0:T(8,128)} %all-reduce.5.cloned.1.call-done), kind=kOutput, calls=%fused_computation.18 | convolution fusion | flops 404783104 | bytes 4456448 | tf_op jit(solution)/shard_map/dot_general | solution.py:59
  50.8 0.0 reduce-scatter.5.cloned.1.call-update
  50.9 0.0 all-reduce.7.cloned.1.call-start
  50.9 0.0 copy-done
  50.9 0.1 fusion.20
  51.1 0.3 fusion.29
  51.3 18.9 %reduce-scatter.5.cloned.1.call-done = f32[32,256]{1,0:T(8,128)} async-done(((f32[32,1024]{1,0:T(8,128)}), f32[32,256]{1,0:T(8,128)}) %reduce-scatter.5.cloned.1.call-update) | async-done | bytes 32784 | tf_op jit(solution)/shard_map/reduce_scatter | solution.py:61
  70.2 0.8 fusion.36
  71.0 13.6 %all_gather.12 = f32[32,1024]{1,0:T(8,128)S(1)} all-gather(f32[32,256]{1,0:T(8,128)S(1)} %fusion.36), channel_id=1, replica_groups=mesh['groups'=2,'cand'=4,'tgt'=2,'mix'=2] {'cand'}, dimensions={1}, use_global_device_ids=true | all-gather | bytes 163840 | tf_op jit(solution)/shard_map/all_gather | solution.py:65
  84.6 6.9 %fusion.13 = f32[32,1024]{1,0:T(8,128)} fusion(f32[32,1024]{1,0:T(8,128)S(1)} %all_gather.12, f32[1024,1024]{1,0:T(8,128)} %copy-done.1), kind=kOutput, calls=%fused_computation.17 | convolution fusion | flops 404750336 | bytes 4456448 | tf_op jit(solution)/shard_map/dot_general | solution.py:55
  91.5 0.0 all-reduce.7.cloned.1.call-update
  91.5 0.0 reduce-scatter.7.cloned.1.call-start
  91.6 19.7 %all-reduce.7.cloned.1.call-done = f32[32,1024]{1,0:T(8,128)} async-done(((f32[32,1024]{1,0:T(8,128)}), f32[32,1024]{1,0:T(8,128)}) %all-reduce.7.cloned.1.call-update) | async-done | bytes 131088 | tf_op jit(solution)/shard_map/psum | solution.py:58
  111.3 5.9 %fusion.12 = f32[32,1024]{1,0:T(8,128)} fusion(f32[1024,1024]{1,0:T(8,128)} %copy-done.1, f32[32,1024]{1,0:T(8,128)} %all-reduce.7.cloned.1.call-done), kind=kOutput, calls=%fused_computation.16 | convolution fusion | flops 404783104 | bytes 4456448 | tf_op jit(solution)/shard_map/dot_general | solution.py:59
  117.2 0.0 reduce-scatter.7.cloned.1.call-update
  117.2 0.0 all-reduce.9.cloned.1.call-start
  117.2 19.3 %reduce-scatter.7.cloned.1.call-done = f32[32,256]{1,0:T(8,128)} async-done(((f32[32,1024]{1,0:T(8,128)}), f32[32,256]{1,0:T(8,128)}) %reduce-scatter.7.cloned.1.call-update) | async-done | bytes 32784 | tf_op jit(solution)/shard_map/reduce_scatter | solution.py:61
  136.5 0.8 fusion.35
  137.4 13.4 %all_gather.13 = f32[32,1024]{1,0:T(8,128)S(1)} all-gather(f32[32,256]{1,0:T(8,128)S(1)} %fusion.35), channel_id=1, replica_groups=mesh['groups'=2,'cand'=4,'tgt'=2,'mix'=2] {'cand'}, dimensions={1}, use_global_device_ids=true | all-gather | bytes 163840 | tf_op jit(solution)/shard_map/all_gather | solution.py:65
  150.7 6.9 %fusion.19 = f32[32,1024]{1,0:T(8,128)} fusion(f32[1024,1024]{1,0:T(8,128)} %copy-done.1, f32[32,1024]{1,0:T(8,128)S(1)} %all_gather.13), kind=kOutput, calls=%fused_computation.23 | convolution fusion | flops 404783104 | bytes 4456448 | tf_op jit(solution)/shard_map/dot_general | solution.py:55
  157.7 0.0 all-reduce.9.cloned.1.call-update
  157.7 0.3 reduce-scatter.9.cloned.1.call-start
  158.0 19.5 %all-reduce.9.cloned.1.call-done = f32[32,1024]{1,0:T(8,128)} async-done(((f32[32,1024]{1,0:T(8,128)}), f32[32,1024]{1,0:T(8,128)}) %all-reduce.9.cloned.1.call-update) | async-done | bytes 131088 | tf_op jit(solution)/shard_map/psum | solution.py:58
  177.5 5.9 %fusion.18 = f32[32,1024]{1,0:T(8,128)} fusion(f32[1024,1024]{1,0:T(8,128)} %copy-done.1, f32[32,1024]{1,0:T(8,128)} %all-reduce.9.cloned.1.call-done), kind=kOutput, calls=%fused_computation.22 | convolution fusion | flops 404783104 | bytes 4456448 | tf_op jit(solution)/shard_map/dot_general | solution.py:59
  183.3 0.0 reduce-scatter.9.cloned.1.call-update
  183.4 0.0 all-reduce.11.cloned.1.call-start
  183.4 19.3 %reduce-scatter.9.cloned.1.call-done = f32[32,256]{1,0:T(8,128)} async-done(((f32[32,1024]{1,0:T(8,128)}), f32[32,256]{1,0:T(8,128)}) %reduce-scatter.9.cloned.1.call-update) | async-done | bytes 32784 | tf_op jit(solution)/shard_map/reduce_scatter | solution.py:61
  202.7 0.8 fusion.34
  203.5 13.4 %all_gather.14 = f32[32,1024]{1,0:T(8,128)S(1)} all-gather(f32[32,256]{1,0:T(8,128)S(1)} %fusion.34), channel_id=1, replica_groups=mesh['groups'=2,'cand'=4,'tgt'=2,'mix'=2] {'cand'}, dimensions={1}, use_global_device_ids=true | all-gather | bytes 163840 | tf_op jit(solution)/shard_map/all_gather | solution.py:65
  216.9 6.9 %fusion.17 = f32[32,1024]{1,0:T(8,128)} fusion(f32[32,1024]{1,0:T(8,128)S(1)} %all_gather.14, f32[1024,1024]{1,0:T(8,128)} %copy-done.1), kind=kOutput, calls=%fused_computation.21 | convolution fusion | flops 404750336 | bytes 4456448 | tf_op jit(solution)/shard_map/dot_general | solution.py:55
  223.8 0.0 all-reduce.11.cloned.1.call-update
  223.9 0.0 reduce-scatter.11.cloned.1.call-start
  223.9 19.7 %all-reduce.11.cloned.1.call-done = f32[32,1024]{1,0:T(8,128)} async-done(((f32[32,1024]{1,0:T(8,128)}), f32[32,1024]{1,0:T(8,128)}) %all-reduce.11.cloned.1.call-update) | async-done | bytes 131088 | tf_op jit(solution)/shard_map/psum | solution.py:58
  243.6 0.0 copy-start.4
  243.6 5.9 %fusion.16 = f32[32,1024]{1,0:T(8,128)} fusion(f32[1024,1024]{1,0:T(8,128)} %copy-done.1, f32[32,1024]{1,0:T(8,128)} %all-reduce.11.cloned.1.call-done), kind=kOutput, calls=%fused_computation.20 | convolution fusion | flops 404783104 | bytes 4456448 | tf_op jit(solution)/shard_map/dot_general | solution.py:59
  249.5 0.0 reduce-scatter.11.cloned.1.call-update
  249.6 0.0 copy-done.4
  249.6 0.7 fusion.30
  250.3 18.6 %reduce-scatter.11.cloned.1.call-done = f32[32,256]{1,0:T(8,128)} async-done(((f32[32,1024]{1,0:T(8,128)}), f32[32,256]{1,0:T(8,128)}) %reduce-scatter.11.cloned.1.call-update) | async-done | bytes 32784 | tf_op jit(solution)/shard_map/reduce_scatter | solution.py:61
  268.9 0.8 fusion.33
  269.8 13.4 %all_gather.15 = f32[32,1024]{1,0:T(8,128)S(1)} all-gather(f32[32,256]{1,0:T(8,128)S(1)} %fusion.33), channel_id=1, replica_groups=mesh['groups'=2,'cand'=4,'tgt'=2,'mix'=2] {'cand'}, dimensions={1}, use_global_device_ids=true | all-gather | bytes 163840 | tf_op jit(solution)/shard_map/all_gather | solution.py:65
  283.1 0.7 log.7
  (2 shorter events, 0.0 us)
Async XLA Ops:
  7.2 43.8 %copy-start = (f32[32,16]{0,1:T(8,128)S(1)}, f32[32,16]{0,1:T(8,128)}, u32[]{:S(2)}) copy-start(f32[32,16]{0,1:T(8,128)} %param.7) | copy-start | bytes 6148
  7.2 4.4 %copy-start.2 = (bf16[1024,1024]{1,0:T(8,128)(2,1)S(1)}, bf16[1024,1024]{1,0:T(8,128)(2,1)}, u32[]{:S(2)}) copy-start(bf16[1024,1024]{1,0:T(8,128)(2,1)} %param.5) | copy-start | bytes 6291460
  7.2 37.8 %all-reduce.5.cloned.1.call-start = ((), (), s32[]{:S(2)}) async-start(), calls=%async_computation.4 | async-start | bytes 262144 | tf_op jit(solution)/shard_map/psum | solution.py:58
  7.2 4.3 %copy-start.3 = (bf16[1024,1024]{1,0:T(8,128)(2,1)S(1)}, bf16[1024,1024]{1,0:T(8,128)(2,1)}, u32[]{:S(2)}) copy-start(bf16[1024,1024]{1,0:T(8,128)(2,1)} %param.4) | copy-start | bytes 6291460
  14.1 1.9 copy-start.1
  16.0 4.7 %copy-start.5 = (s32[2048]{0:T(1024)S(1)}, s32[2048]{0:T(1024)}, u32[]{:S(2)}) copy-start(s32[2048]{0:T(1024)} %param.6) | copy-start | bytes 24580
  20.7 49.5 %reduce-scatter.5.cloned.1.call-start = ((), (), s32[]{:S(2)}) async-start(), calls=%async_computation.5 | async-start | bytes 163840 | tf_op jit(solution)/shard_map/reduce_scatter | solution.py:61
  50.9 60.4 %all-reduce.7.cloned.1.call-start = ((), (), s32[]{:S(2)}) async-start(), calls=%async_computation.6 | async-start | bytes 262144 | tf_op jit(solution)/shard_map/psum | solution.py:58
  91.5 45.0 %reduce-scatter.7.cloned.1.call-start = ((), (), s32[]{:S(2)}) async-start(), calls=%async_computation.7 | async-start | bytes 163840 | tf_op jit(solution)/shard_map/reduce_scatter | solution.py:61
  117.2 60.3 %all-reduce.9.cloned.1.call-start = ((), (), s32[]{:S(2)}) async-start(), calls=%async_computation.8 | async-start | bytes 262144 | tf_op jit(solution)/shard_map/psum | solution.py:58
  157.7 45.0 %reduce-scatter.9.cloned.1.call-start = ((), (), s32[]{:S(2)}) async-start(), calls=%async_computation.9 | async-start | bytes 163840 | tf_op jit(solution)/shard_map/reduce_scatter | solution.py:61
  183.4 60.3 %all-reduce.11.cloned.1.call-start = ((), (), s32[]{:S(2)}) async-start(), calls=%async_computation.10 | async-start | bytes 262144 | tf_op jit(solution)/shard_map/psum | solution.py:58
  223.9 45.1 %reduce-scatter.11.cloned.1.call-start = ((), (), s32[]{:S(2)}) async-start(), calls=%async_computation.11 | async-start | bytes 163840 | tf_op jit(solution)/shard_map/reduce_scatter | solution.py:61
  243.6 5.9 %copy-start.4 = (f32[32,1024]{1,0:T(8,128)S(1)}, f32[32,1024]{1,0:T(8,128)}, u32[]{:S(2)}) copy-start(f32[32,1024]{1,0:T(8,128)} %all-reduce.11.cloned.1.call-done) | copy-start | bytes 393220
Sparse Core Ops, SparseCore 0:
  20.8 24.0 all-reduce.4
  51.0 19.1 reduce-scatter.4
  91.7 19.5 all-reduce.6
  117.3 19.1 reduce-scatter.6
  157.8 19.6 all-reduce.8
  183.5 19.1 reduce-scatter.8
  224.0 19.6 all-reduce.10
  249.7 19.1 reduce-scatter.10
where the time goes:
time: 291 us
  waiting for transfers between devices  159 us (55%)
  blocking collectives  53.7 us (18%)
  matrix products  51.8 us (18%)
  between operations  14.2 us (5%)
  other arithmetic  8.44 us (3%)
    psum x4, waiting for transfers between devices, local(): scale_cand = 1.0 / lax.psum(partial_value, 'tgt')  83 us
    reduce_scatter x4, waiting for transfers between devices, local(): lax.psum_scatter(column_part, 'cand', scatter_dimension=1, tiled=True)  76.1 us
    all_gather x4, blocking collectives, local(): scale_tgt = lax.all_gather(own_mass / summed, 'cand', axis=1, tiled=True)  53.7 us
    dot_general x4, matrix products, local(): lax.dot_general(scale_tgt, kernel, (((1,), (1,)), ((), ())), precision=la...  25.4 us
    dot_general x4, matrix products, local(): column_part = jnp.dot(scale_cand, kernel, precision=lax.Precision.HIGHEST)  23.5 us
  transfers between devices with their start and end apart: 8, of which 8 were waited for; matrix products, arithmetic and copies ran while one was open for 0% of the time, Pallas kernels for 0%

commit v1 on v0

--- a/solution.py
+++ b/solution.py
@@ -1,8 +1,11 @@
+import functools
 import math
 
 import jax
 import jax.numpy as jnp
 from jax import lax
+from jax.experimental import pallas as pl
+from jax.experimental.pallas import tpu as pltpu
 from jax.sharding import PartitionSpec as P
 
 ITERS = 2
@@ -10,6 +13,12 @@
 
 EPS_FIRST = 0.05
 EPS_SECOND = 0.025
+
+MESH = pl.DeviceIdType.MESH
+F32 = jnp.float32
+BF16 = jnp.bfloat16
+NT_DIMS = (((1,), (1,)), ((), ()))
+NN_DIMS = (((1,), (0,)), ((), ()))
 
 
 def unit_rows(embedding):
@@ -21,9 +30,230 @@
 
 
 def contract_last(left, right):
-    return lax.dot_general(
-        left, right, (((1,), (1,)), ((), ())), preferred_element_type=jnp.float32
-    )
+    return lax.dot_general(left, right, NT_DIMS, preferred_element_type=jnp.float32)
+
+
+def split_rows(value):
+    head = value.astype(BF16)
+    rest = (value - head.astype(F32)).astype(BF16)
+    return jnp.concatenate([head, rest], axis=0)
+
+
+def join_rows(value):
+    half = value.shape[0] // 2
+    return value[:half] + value[half:]
+
+
+def fused_kernel(
+    n_tgt, n_cand, cand_ref, tgt_ref, member_ref, weight_ref, out_cand, out_tgt,
+    tgt_unit, k_one, k_two, mass, acc,
+    row_slots, col_slots, task_slots, cand_slots, rs_send, rs_slots, ag_slots,
+    x_send, x_recv, z_send, z_recv,
+):
+    xi, zi = lax.axis_index("tgt"), lax.axis_index("cand")
+    rows, width = cand_ref.shape
+    cols = tgt_ref.shape[0]
+    mixes, tasks = weight_ref.shape
+    share = cols // n_cand
+    tgt_total, cand_total = cols * n_tgt, rows * n_cand
+
+    def x_peer(d):
+        return {"tgt": lax.rem(xi + d, n_tgt)}
+
+    def z_peer(d):
+        return {"cand": lax.rem(zi + d, n_cand)}
+
+    barrier = pltpu.get_barrier_semaphore()
+    for d in range(1, n_tgt):
+        pl.semaphore_signal(barrier, inc=1, device_id=x_peer(d), device_id_type=MESH)
+    for d in range(1, n_cand):
+        pl.semaphore_signal(barrier, inc=1, device_id=z_peer(d), device_id_type=MESH)
+
+    def send(src, dst, sems, phase, d, peer):
+        copy = pltpu.make_async_remote_copy(
+            src_ref=src, dst_ref=dst,
+            send_sem=sems[0].at[phase, d - 1], recv_sem=sems[1].at[phase, d - 1],
+            device_id=peer, device_id_type=MESH,
+        )
+        copy.start()
+        pending.append(copy)
+        return copy
+
+    pending = []
+    xs, zs = (x_send, x_recv), (z_send, z_recv)
+
+    def x_sum(slots):
+        total = slots[lax.rem(xi + n_tgt, n_tgt)]
+        for k in range(1, n_tgt):
+            total = total + slots[lax.rem(xi - k + n_tgt, n_tgt)]
+        return total
+
+    def z_sum(slots):
+        total = slots[lax.rem(zi + n_cand, n_cand)]
+        for k in range(1, n_cand):
+            total = total + slots[lax.rem(zi - k + n_cand, n_cand)]
+        return total
+
+    def x_exchange(slots, phase):
+        copies = [send(slots.at[0], slots.at[d], xs, phase, d, x_peer(d)) for d in range(1, n_tgt)]
+        for copy in copies:
+            copy.wait_recv()
+        return x_sum(slots)
+
+    block = 256
+
+    def norm_targets(b, carry):
+        at = pl.ds(pl.multiple_of(b * block, block), block)
+        tgt_unit[at, :] = unit_rows(tgt_ref[at, :])
+        return carry
+
+    lax.fori_loop(0, cols // block, norm_targets, 0)
+
+    def build(b, carry):
+        at = pl.ds(pl.multiple_of(b * block, block), block)
+        scores = contract_last(unit_rows(cand_ref[at, :]), tgt_unit[...])
+        raised = jnp.exp(scores * (1.0 / EPS_FIRST))
+        k_one[at, :] = (raised * (1.0 / tgt_total)).astype(BF16)
+        k_two[at, :] = (raised * raised * (1.0 / tgt_total)).astype(BF16)
+        return carry
+
+    lax.fori_loop(0, rows // block, build, 0)
+
+    all_ids = lax.broadcasted_iota(jnp.int32, (tasks, tgt_total), 0)
+    all_hot = (member_ref[...] == all_ids).astype(F32)
+    weights = weight_ref[...]
+    per_target = lax.dot_general(
+        weights, all_hot, NN_DIMS, precision=lax.Precision.HIGHEST, preferred_element_type=F32
+    )
+    ratio = float(cand_total) / jnp.sum(per_target, axis=1, keepdims=True)
+    own = pl.ds(pl.multiple_of(xi * cols, cols), cols)
+    own_hot = (
+        member_ref[:, own] == lax.broadcasted_iota(jnp.int32, (tasks, cols), 0)
+    ).astype(F32)
+    mass[...] = (
+        lax.dot_general(
+            weights, own_hot, NN_DIMS, precision=lax.Precision.HIGHEST, preferred_element_type=F32
+        )
+        * ratio
+    )
+
+    pl.semaphore_wait(barrier, n_tgt - 1 + n_cand - 1)
+
+    ones = jnp.ones((16, cols), BF16)
+    row_slots[0] = contract_last(ones, k_one[...])[:1]
+    scale_row = 1.0 / x_exchange(row_slots, 0)
+    place = lax.broadcasted_iota(jnp.int32, (16, rows), 0)
+    head = scale_row.astype(BF16).astype(F32)
+    lhs = jnp.where(place == 0, head, jnp.where(place == 1, scale_row - head, 0.0)).astype(BF16)
+    part = lax.dot_general(lhs, k_one[...], NN_DIMS, preferred_element_type=F32)
+    col_slots[0] = part[:1] + part[1:2]
+    copies = [
+        send(col_slots.at[0], col_slots.at[d], zs, 0, d, z_peer(d)) for d in range(1, n_cand)
+    ]
+    for copy in copies:
+        copy.wait_recv()
+    col_sum = z_sum(col_slots)
+
+    task_slots[0] = join_rows(contract_last(split_rows(own_hot / col_sum), k_one[...]))
+    by_task = x_exchange(task_slots, 1)
+    cand_sum = ratio * lax.dot_general(
+        weights, by_task, NN_DIMS, precision=lax.Precision.HIGHEST, preferred_element_type=F32
+    )
+
+    def tgt_pass(cand_sum, kernel, turn):
+        lhs = split_rows(1.0 / cand_sum)
+
+        def columns(peer):
+            at = pl.ds(pl.multiple_of(peer * share, share), share)
+            return join_rows(
+                lax.dot_general(lhs, kernel[:, at], NN_DIMS, preferred_element_type=F32)
+            )
+
+        copies = []
+        for d in range(1, n_cand):
+            rs_send[turn, d - 1] = columns(lax.rem(zi + d, n_cand))
+            copies.append(
+                send(rs_send.at[turn, d - 1], rs_slots.at[turn, d], zs, 1 + 2 * turn, d, z_peer(d))
+            )
+        rs_slots[turn, 0] = columns(zi)
+        for copy in copies:
+            copy.wait_recv()
+        total = z_sum(rs_slots.at[turn])
+        at = pl.ds(pl.multiple_of(zi * share, share), share)
+        return mass[:, at] / total
+
+    def gather(value, turn):
+        ag_slots[turn, 0] = value
+        return [
+            send(ag_slots.at[turn, 0], ag_slots.at[turn, d], zs, 2 + 2 * turn, d, z_peer(d))
+            for d in range(1, n_cand)
+        ]
+
+    def cand_pass(copies, turn):
+        for d in range(n_cand):
+            if d:
+                copies[d - 1].wait_recv()
+            at = pl.ds(pl.multiple_of(lax.rem(zi - d + n_cand, n_cand) * share, share), share)
+            part = contract_last(split_rows(ag_slots[turn, d]), k_two[:, at])
+            if d:
+                acc[...] += part
+            else:
+                acc[...] = part
+        cand_slots[turn, 0] = join_rows(acc[...])
+        return x_exchange(cand_slots.at[turn], 2 + turn)
+
+    scale = tgt_pass(cand_sum, k_one, 0)
+    scale = scale * scale
+    for repeat in range(ITERS):
+        cand_sum = cand_pass(gather(scale, repeat), repeat)
+        scale = tgt_pass(cand_sum, k_two, 1 + repeat)
+    copies = gather(jnp.log(scale), ITERS)
+    out_cand[...] = -jnp.log(cand_sum)
+    for d in range(n_cand):
+        if d:
+            copies[d - 1].wait_recv()
+        at = pl.ds(pl.multiple_of(lax.rem(zi - d + n_cand, n_cand) * share, share), share)
+        out_tgt[:, at] = ag_slots[ITERS, d]
+    for copy in pending:
+        copy.wait_send()
+
+
+def fused(candidates, targets, member, mix_weight):
+    n_tgt, n_cand = lax.axis_size("tgt"), lax.axis_size("cand")
+    rows, width = candidates.shape
+    cols = targets.shape[0]
+    mixes, tasks = mix_weight.shape
+    share = cols // n_cand
+    return tuple(pl.pallas_call(
+        functools.partial(fused_kernel, n_tgt, n_cand),
+        out_shape=(
+            jax.ShapeDtypeStruct((mixes, rows), F32),
+            jax.ShapeDtypeStruct((mixes, cols), F32),
+        ),
+        in_specs=[pl.BlockSpec(memory_space=pltpu.VMEM)] * 4,
+        out_specs=(pl.BlockSpec(memory_space=pltpu.VMEM),) * 2,
+        scratch_shapes=[
+            pltpu.VMEM((cols, width), BF16),
+            pltpu.VMEM((rows, cols), BF16),
+            pltpu.VMEM((rows, cols), BF16),
+            pltpu.VMEM((mixes, cols), F32),
+            pltpu.VMEM((2 * mixes, rows), F32),
+            pltpu.VMEM((n_tgt, 1, rows), F32),
+            pltpu.VMEM((n_cand, 1, cols), F32),
+            pltpu.VMEM((n_tgt, tasks, rows), F32),
+            pltpu.VMEM((ITERS, n_tgt, mixes, rows), F32),
+            pltpu.VMEM((1 + ITERS, n_cand - 1, mixes, share), F32),
+            pltpu.VMEM((1 + ITERS, n_cand, mixes, share), F32),
+            pltpu.VMEM((1 + ITERS, n_cand, mixes, share), F32),
+            pltpu.SemaphoreType.DMA((2 + ITERS, n_tgt - 1)),
+            pltpu.SemaphoreType.DMA((2 + ITERS, n_tgt - 1)),
+            pltpu.SemaphoreType.DMA((3 + 2 * ITERS, n_cand - 1)),
+            pltpu.SemaphoreType.DMA((3 + 2 * ITERS, n_cand - 1)),
+        ],
+        compiler_params=pltpu.CompilerParams(
+            collective_id=0, has_side_effects=True, vmem_limit_bytes=48 * 1024 * 1024
+        ),
+    )(candidates, targets, member.reshape(1, -1), mix_weight))
 
 
 def target_mass(own_member, member, mix_weight, cand_total):
@@ -35,7 +265,7 @@
     return per_target * (cand_total / weight_total)[:, None]
 
 
-def local(candidates, targets, member, mix_weight):
+def by_collectives(candidates, targets, member, mix_weight):
     cand_rows = candidates.shape[0]
     tgt_rows = targets.shape[0]
     tgt_total = tgt_rows * lax.axis_size("tgt")
@@ -74,4 +304,11 @@
         P("mix", "groups"),
     )
     out_specs = (P("mix", ("groups", "cand")), P("mix", ("groups", "tgt")))
+    n_tgt, n_cand = mesh.shape["tgt"], mesh.shape["cand"]
+
+    def local(candidates, targets, member, mix_weight):
+        lanes = targets.shape[0] % (128 * n_cand) == 0
+        step = fused if lanes and n_cand > 1 and n_tgt > 1 else by_collectives
+        return step(candidates, targets, member, mix_weight)
+
     return jax.shard_map(local, mesh=mesh, in_specs=in_specs, out_specs=out_specs, check_vma=False)

time: 291 us -> 62.3 us (0.21)
  waiting for transfers between devices: 159 us -> 0 us
  Pallas kernels: 0 us -> 55.4 us
  blocking collectives: 53.7 us -> 0 us
  matrix products: 51.8 us -> 0 us
  between operations: 14.2 us -> 0.64 us
  other arithmetic: 8.44 us -> 0 us
  local copies, waits for them, and re-layouts: 2.63 us -> 5.96 us
    psum x4 -> x0, waiting for transfers between devices: 83 us -> none  [local(): scale_cand = 1.0 / lax.psum(partial_value, 'tgt')]
    reduce_scatter x4 -> x0, waiting for transfers between devices: 76.1 us -> none  [local(): lax.psum_scatter(column_part, 'cand', scatter_dimension=1, tiled=True)]
    pallas_call x0 -> x1, Pallas kernels: none -> 55.4 us  [fused(): pl.pallas_call(functools.partial(fused_kernel, n_tgt, n_cand), out_shape=...]
    all_gather x4 -> x0, blocking collectives: 53.7 us -> none  [local(): scale_tgt = lax.all_gather(own_mass / summed, 'cand', axis=1, tiled=True)]
    dot_general x11 -> x0, matrix products: 51.8 us -> none  [the longest x4 25.4 us: local(): lax.dot_general(scale_tgt, kernel, (((1,), (1,)), ((), ())), precision=la...]
    reduce_sum x3 -> x0, other arithmetic: 4.42 us -> none  [the longest x2 4.29 us: unit_rows(): mean_sq = jnp.mean(values * values, axis=1, keepdims=True)]
    unnamed x12 -> x9, local copies, waits for them, and re-layouts: 1.95 us -> 5.96 us
    div x4 -> x0, other arithmetic: 3.32 us -> none  [local(): scale_tgt = lax.all_gather(own_mass / summed, 'cand', axis=1, tiled=True)]
  transfers between devices with their start and end apart: 8 -> 0, of which waited for: 8 -> 0; matrix products, arithmetic and copies ran while one was open for 0% -> 0% of each run, Pallas kernels for 0% -> 0%
where the time goes in v1:
time: 62.3 us; the launch traced here: 62 us
  Pallas kernels  55.4 us (89%)
  local copies, waits for them, and re-layouts  5.96 us (10%)
  between operations  0.64 us (1%)
    pallas_call x1, Pallas kernels, fused(): pl.pallas_call(functools.partial(fused_kernel, n_tgt, n_cand), out_shape=...  55.4 us
    unnamed x9, local copies, waits for them, and re-layouts  5.96 us

profile of v1, /device:TPU:0, one launch (start us, length us, event | category | flops | bytes accessed | tf_op | source)
XLA Modules:
  0.0 62.0 jit_solution(1859806620787379064)
XLA Ops:
  0.6 0.8 %copy.6.weight_ref = f32[32,16]{1,0:T(8,128)S(1)} copy(f32[32,16]{0,1:T(8,128)} %param.7) | data formatting | bytes 4096 | tf_op args[3]
  1.4 0.0 copy-start
  1.4 1.6 %copy-done = bf16[1024,1024]{1,0:T(8,128)(2,1)S(1)} copy-done((bf16[1024,1024]{1,0:T(8,128)(2,1)S(1)}, bf16[1024,1024]{1,0:T(8,128)(2,1)}, u32[]{:S(2)}) %copy-start) | copy-done | bytes 2097176
  3.0 0.0 copy-start.1
  3.0 1.6 %copy-done.1 = bf16[1024,1024]{1,0:T(8,128)(2,1)S(1)} copy-done((bf16[1024,1024]{1,0:T(8,128)(2,1)S(1)}, bf16[1024,1024]{1,0:T(8,128)(2,1)}, u32[]{:S(2)}) %copy-start.1) | copy-done | bytes 2097176
  4.6 0.0 copy-start.2
  4.6 0.7 %copy-done.2 = s32[2048]{0:T(1024)S(1)} copy-done((s32[2048]{0:T(1024)S(1)}, s32[2048]{0:T(1024)}, u32[]{:S(2)}) %copy-start.2) | copy-done | bytes 8216
  5.3 55.4 %shard_map.59 = (f32[32,1024]{1,0:T(8,128)S(1)}, f32[32,1024]{1,0:T(8,128)S(1)}) custom-call(bf16[1024,1024]{1,0:T(8,128)(2,1)S(1)} %copy-done, bf16[1024,1024]{1,0:T(8,128)(2,1)S(1)} %copy-done.1, s32[1,2048]{1,0:T(1,128)S(1)} %bitcast.1, f32[32,16]{1,0:T(8,128)S(1)} %copy.6.weight_ref), custom_call_target="tpu_custom_call" | custom-call | tf_op jit(solution)/shard_map/pallas_call | solution.py:227
  60.7 0.7 %copy.9 = f32[32,1024]{1,0:T(8,128)} copy(f32[32,1024]{1,0:T(8,128)S(1)} %get-tuple-element.4) | data formatting | bytes 262144
  61.3 0.7 %copy.10 = f32[32,1024]{1,0:T(8,128)} copy(f32[32,1024]{1,0:T(8,128)S(1)} %get-tuple-element.5) | data formatting | bytes 262144
Async XLA Ops:
  1.4 1.6 %copy-start = (bf16[1024,1024]{1,0:T(8,128)(2,1)S(1)}, bf16[1024,1024]{1,0:T(8,128)(2,1)}, u32[]{:S(2)}) copy-start(bf16[1024,1024]{1,0:T(8,128)(2,1)} %cand_ref.1) | copy-start | bytes 6291460
  3.0 1.6 %copy-start.1 = (bf16[1024,1024]{1,0:T(8,128)(2,1)S(1)}, bf16[1024,1024]{1,0:T(8,128)(2,1)}, u32[]{:S(2)}) copy-start(bf16[1024,1024]{1,0:T(8,128)(2,1)} %tgt_ref.1) | copy-start | bytes 6291460
  4.6 0.7 %copy-start.2 = (s32[2048]{0:T(1024)S(1)}, s32[2048]{0:T(1024)}, u32[]{:S(2)}) copy-start(s32[2048]{0:T(1024)} %param.6) | copy-start | bytes 24580

commit v2 on v1

--- a/solution.py
+++ b/solution.py
@@ -45,17 +45,31 @@
 
 
 def fused_kernel(
-    n_tgt, n_cand, cand_ref, tgt_ref, member_ref, weight_ref, out_cand, out_tgt,
-    tgt_unit, k_one, k_two, mass, acc,
+    n_tgt, n_cand, parts, cand_hbm, tgt_hbm, member_ref, weight_ref, out_cand, out_tgt,
+    cand_rows, tgt_rows, tgt_unit, raised, k_one, k_two, mass, cand_sums,
     row_slots, col_slots, task_slots, cand_slots, rs_send, rs_slots, ag_slots,
-    x_send, x_recv, z_send, z_recv,
+    load_sems, x_send, x_recv, z_send, z_recv,
 ):
     xi, zi = lax.axis_index("tgt"), lax.axis_index("cand")
-    rows, width = cand_ref.shape
-    cols = tgt_ref.shape[0]
+    rows, width = cand_hbm.shape
+    cols = tgt_hbm.shape[0]
     mixes, tasks = weight_ref.shape
     share = cols // n_cand
+    group = mixes // parts
     tgt_total, cand_total = cols * n_tgt, rows * n_cand
+    block = 256
+
+    def loads(src, dst, row):
+        return [
+            pltpu.make_async_copy(
+                src.at[pl.ds(at, block)], dst.at[pl.ds(at, block)], load_sems.at[row, at // block]
+            )
+            for at in range(0, src.shape[0], block)
+        ]
+
+    tgt_loads, cand_loads = loads(tgt_hbm, tgt_rows, 0), loads(cand_hbm, cand_rows, 1)
+    for copy in tgt_loads + cand_loads:
+        copy.start()
 
     def x_peer(d):
         return {"tgt": lax.rem(xi + d, n_tgt)}
@@ -68,6 +82,9 @@
         pl.semaphore_signal(barrier, inc=1, device_id=x_peer(d), device_id_type=MESH)
     for d in range(1, n_cand):
         pl.semaphore_signal(barrier, inc=1, device_id=z_peer(d), device_id_type=MESH)
+
+    pending = []
+    xs, zs = (x_send, x_recv), (z_send, z_recv)
 
     def send(src, dst, sems, phase, d, peer):
         copy = pltpu.make_async_remote_copy(
@@ -79,9 +96,6 @@
         pending.append(copy)
         return copy
 
-    pending = []
-    xs, zs = (x_send, x_recv), (z_send, z_recv)
-
     def x_sum(slots):
         total = slots[lax.rem(xi + n_tgt, n_tgt)]
         for k in range(1, n_tgt):
@@ -94,30 +108,19 @@
             total = total + slots[lax.rem(zi - k + n_cand, n_cand)]
         return total
 
-    def x_exchange(slots, phase):
-        copies = [send(slots.at[0], slots.at[d], xs, phase, d, x_peer(d)) for d in range(1, n_tgt)]
+    def x_start(slots, phase):
+        return [send(slots.at[0], slots.at[d], xs, phase, d, x_peer(d)) for d in range(1, n_tgt)]
+
+    def z_start(slots, phase):
+        return [send(slots.at[0], slots.at[d], zs, phase, d, z_peer(d)) for d in range(1, n_cand)]
+
+    def arrive(copies):
         for copy in copies:
             copy.wait_recv()
-        return x_sum(slots)
-
-    block = 256
-
-    def norm_targets(b, carry):
-        at = pl.ds(pl.multiple_of(b * block, block), block)
-        tgt_unit[at, :] = unit_rows(tgt_ref[at, :])
-        return carry
-
-    lax.fori_loop(0, cols // block, norm_targets, 0)
-
-    def build(b, carry):
-        at = pl.ds(pl.multiple_of(b * block, block), block)
-        scores = contract_last(unit_rows(cand_ref[at, :]), tgt_unit[...])
-        raised = jnp.exp(scores * (1.0 / EPS_FIRST))
-        k_one[at, :] = (raised * (1.0 / tgt_total)).astype(BF16)
-        k_two[at, :] = (raised * raised * (1.0 / tgt_total)).astype(BF16)
-        return carry
-
-    lax.fori_loop(0, rows // block, build, 0)
+
+    def z_columns(d):
+        at = lax.rem(zi - d + n_cand, n_cand) * share
+        return pl.ds(pl.multiple_of(at, share), share)
 
     all_ids = lax.broadcasted_iota(jnp.int32, (tasks, tgt_total), 0)
     all_hot = (member_ref[...] == all_ids).astype(F32)
@@ -137,31 +140,57 @@
         * ratio
     )
 
+    for index, copy in enumerate(tgt_loads):
+        copy.wait()
+        at = pl.ds(index * block, block)
+        tgt_unit[at, :] = unit_rows(tgt_rows[at, :])
+    for index, copy in enumerate(cand_loads):
+        copy.wait()
+        at = pl.ds(index * block, block)
+        scores = contract_last(unit_rows(cand_rows[at, :]), tgt_unit[...])
+        power = jnp.exp(scores * (1.0 / EPS_FIRST))
+        raised[at, :] = power
+        k_one[at, :] = (power * (1.0 / tgt_total)).astype(BF16)
+
+    def square(first, last):
+        def step(b, carry):
+            at = pl.ds(pl.multiple_of(b * 64, 64), 64)
+            power = raised[at, :]
+            k_two[at, :] = (power * power * (1.0 / tgt_total)).astype(BF16)
+            return carry
+
+        lax.fori_loop(first // 64, last // 64, step, 0)
+
     pl.semaphore_wait(barrier, n_tgt - 1 + n_cand - 1)
 
     ones = jnp.ones((16, cols), BF16)
     row_slots[0] = contract_last(ones, k_one[...])[:1]
-    scale_row = 1.0 / x_exchange(row_slots, 0)
+    copies = x_start(row_slots, 0)
+    square(0, rows // 2)
+    arrive(copies)
+    scale_row = 1.0 / x_sum(row_slots)
     place = lax.broadcasted_iota(jnp.int32, (16, rows), 0)
     head = scale_row.astype(BF16).astype(F32)
     lhs = jnp.where(place == 0, head, jnp.where(place == 1, scale_row - head, 0.0)).astype(BF16)
     part = lax.dot_general(lhs, k_one[...], NN_DIMS, preferred_element_type=F32)
     col_slots[0] = part[:1] + part[1:2]
-    copies = [
-        send(col_slots.at[0], col_slots.at[d], zs, 0, d, z_peer(d)) for d in range(1, n_cand)
-    ]
-    for copy in copies:
-        copy.wait_recv()
+    copies = z_start(col_slots, 0)
+    square(rows // 2, rows)
+    arrive(copies)
     col_sum = z_sum(col_slots)
 
     task_slots[0] = join_rows(contract_last(split_rows(own_hot / col_sum), k_one[...]))
-    by_task = x_exchange(task_slots, 1)
-    cand_sum = ratio * lax.dot_general(
-        weights, by_task, NN_DIMS, precision=lax.Precision.HIGHEST, preferred_element_type=F32
-    )
-
-    def tgt_pass(cand_sum, kernel, turn):
-        lhs = split_rows(1.0 / cand_sum)
+    arrive(x_start(task_slots, 1))
+    cand_sums[...] = ratio * lax.dot_general(
+        weights, x_sum(task_slots), NN_DIMS, precision=lax.Precision.HIGHEST,
+        preferred_element_type=F32,
+    )
+
+    def of(part):
+        return pl.ds(part * group, group)
+
+    def tgt_send(kernel, turn, part):
+        lhs = split_rows(1.0 / cand_sums[of(part), :])
 
         def columns(peer):
             at = pl.ds(pl.multiple_of(peer * share, share), share)
@@ -169,51 +198,56 @@
                 lax.dot_general(lhs, kernel[:, at], NN_DIMS, preferred_element_type=F32)
             )
 
+        out, slots = rs_send.at[turn, part], rs_slots.at[turn, part]
         copies = []
         for d in range(1, n_cand):
-            rs_send[turn, d - 1] = columns(lax.rem(zi + d, n_cand))
+            out[d - 1] = columns(lax.rem(zi + d, n_cand))
             copies.append(
-                send(rs_send.at[turn, d - 1], rs_slots.at[turn, d], zs, 1 + 2 * turn, d, z_peer(d))
-            )
-        rs_slots[turn, 0] = columns(zi)
-        for copy in copies:
-            copy.wait_recv()
-        total = z_sum(rs_slots.at[turn])
-        at = pl.ds(pl.multiple_of(zi * share, share), share)
-        return mass[:, at] / total
-
-    def gather(value, turn):
-        ag_slots[turn, 0] = value
-        return [
-            send(ag_slots.at[turn, 0], ag_slots.at[turn, d], zs, 2 + 2 * turn, d, z_peer(d))
-            for d in range(1, n_cand)
-        ]
-
-    def cand_pass(copies, turn):
+                send(out.at[d - 1], slots.at[d], zs, 1 + turn * parts + part, d, z_peer(d))
+            )
+        slots[0] = columns(zi)
+        return copies
+
+    def tgt_finish(copies, turn, part, change):
+        arrive(copies)
+        slots = ag_slots.at[turn, part]
+        slots[0] = change(mass[of(part), z_columns(0)] / z_sum(rs_slots.at[turn, part]))
+        return z_start(slots, 1 + (1 + ITERS + turn) * parts + part)
+
+    def cand_send(copies, turn, part):
+        total = None
         for d in range(n_cand):
             if d:
                 copies[d - 1].wait_recv()
-            at = pl.ds(pl.multiple_of(lax.rem(zi - d + n_cand, n_cand) * share, share), share)
-            part = contract_last(split_rows(ag_slots[turn, d]), k_two[:, at])
+            value = contract_last(split_rows(ag_slots[turn, part, d]), k_two[:, z_columns(d)])
+            total = value if total is None else total + value
+        cand_slots[turn, part, 0] = join_rows(total)
+        return x_start(cand_slots.at[turn, part], 2 + turn * parts + part)
+
+    def cand_finish(copies, turn, part):
+        arrive(copies)
+        cand_sums[of(part), :] = x_sum(cand_slots.at[turn, part])
+
+    def keep(scale):
+        return scale
+
+    each = range(parts)
+    reduced = [tgt_send(k_one, 0, part) for part in each]
+    changes = (jnp.square,) + (keep,) * (ITERS - 1)
+    for turn in range(ITERS):
+        gathered = [tgt_finish(reduced[part], turn, part, changes[turn]) for part in each]
+        summed = [cand_send(gathered[part], turn, part) for part in each]
+        reduced = []
+        for part in each:
+            cand_finish(summed[part], turn, part)
+            reduced.append(tgt_send(k_two, 1 + turn, part))
+    out_cand[...] = -jnp.log(cand_sums[...])
+    gathered = [tgt_finish(reduced[part], ITERS, part, jnp.log) for part in each]
+    for part in each:
+        for d in range(n_cand):
             if d:
-                acc[...] += part
-            else:
-                acc[...] = part
-        cand_slots[turn, 0] = join_rows(acc[...])
-        return x_exchange(cand_slots.at[turn], 2 + turn)
-
-    scale = tgt_pass(cand_sum, k_one, 0)
-    scale = scale * scale
-    for repeat in range(ITERS):
-        cand_sum = cand_pass(gather(scale, repeat), repeat)
-        scale = tgt_pass(cand_sum, k_two, 1 + repeat)
-    copies = gather(jnp.log(scale), ITERS)
-    out_cand[...] = -jnp.log(cand_sum)
-    for d in range(n_cand):
-        if d:
-            copies[d - 1].wait_recv()
-        at = pl.ds(pl.multiple_of(lax.rem(zi - d + n_cand, n_cand) * share, share), share)
-        out_tgt[:, at] = ag_slots[ITERS, d]
+                gathered[part][d - 1].wait_recv()
+            out_tgt[of(part), z_columns(d)] = ag_slots[ITERS, part, d]
     for copy in pending:
         copy.wait_send()
 
@@ -224,34 +258,41 @@
     cols = targets.shape[0]
     mixes, tasks = mix_weight.shape
     share = cols // n_cand
+    parts = 2 if mixes % 16 == 0 else 1
+    group = mixes // parts
     return tuple(pl.pallas_call(
-        functools.partial(fused_kernel, n_tgt, n_cand),
+        functools.partial(fused_kernel, n_tgt, n_cand, parts),
         out_shape=(
             jax.ShapeDtypeStruct((mixes, rows), F32),
             jax.ShapeDtypeStruct((mixes, cols), F32),
         ),
-        in_specs=[pl.BlockSpec(memory_space=pltpu.VMEM)] * 4,
+        in_specs=[pl.BlockSpec(memory_space=pltpu.HBM)] * 2
+        + [pl.BlockSpec(memory_space=pltpu.VMEM)] * 2,
         out_specs=(pl.BlockSpec(memory_space=pltpu.VMEM),) * 2,
         scratch_shapes=[
+            pltpu.VMEM((rows, width), BF16),
             pltpu.VMEM((cols, width), BF16),
+            pltpu.VMEM((cols, width), BF16),
+            pltpu.VMEM((rows, cols), F32),
             pltpu.VMEM((rows, cols), BF16),
             pltpu.VMEM((rows, cols), BF16),
             pltpu.VMEM((mixes, cols), F32),
-            pltpu.VMEM((2 * mixes, rows), F32),
+            pltpu.VMEM((mixes, rows), F32),
             pltpu.VMEM((n_tgt, 1, rows), F32),
             pltpu.VMEM((n_cand, 1, cols), F32),
             pltpu.VMEM((n_tgt, tasks, rows), F32),
-            pltpu.VMEM((ITERS, n_tgt, mixes, rows), F32),
-            pltpu.VMEM((1 + ITERS, n_cand - 1, mixes, share), F32),
-            pltpu.VMEM((1 + ITERS, n_cand, mixes, share), F32),
-            pltpu.VMEM((1 + ITERS, n_cand, mixes, share), F32),
-            pltpu.SemaphoreType.DMA((2 + ITERS, n_tgt - 1)),
-            pltpu.SemaphoreType.DMA((2 + ITERS, n_tgt - 1)),
-            pltpu.SemaphoreType.DMA((3 + 2 * ITERS, n_cand - 1)),
-            pltpu.SemaphoreType.DMA((3 + 2 * ITERS, n_cand - 1)),
+            pltpu.VMEM((ITERS, parts, n_tgt, group, rows), F32),
+            pltpu.VMEM((1 + ITERS, parts, n_cand - 1, group, share), F32),
+            pltpu.VMEM((1 + ITERS, parts, n_cand, group, share), F32),
+            pltpu.VMEM((1 + ITERS, parts, n_cand, group, share), F32),
+            pltpu.SemaphoreType.DMA((2, max(rows, cols) // 256)),
+            pltpu.SemaphoreType.DMA((2 + ITERS * parts, n_tgt - 1)),
+            pltpu.SemaphoreType.DMA((2 + ITERS * parts, n_tgt - 1)),
+            pltpu.SemaphoreType.DMA((1 + 2 * (1 + ITERS) * parts, n_cand - 1)),
+            pltpu.SemaphoreType.DMA((1 + 2 * (1 + ITERS) * parts, n_cand - 1)),
         ],
         compiler_params=pltpu.CompilerParams(
-            collective_id=0, has_side_effects=True, vmem_limit_bytes=48 * 1024 * 1024
+            collective_id=0, has_side_effects=True, vmem_limit_bytes=56 * 1024 * 1024
         ),
     )(candidates, targets, member.reshape(1, -1), mix_weight))
 

time: 62.3 us -> 60.8 us (0.976)
  local copies, waits for them, and re-layouts: 5.96 us -> 4.51 us
    unnamed x9 -> x3, local copies, waits for them, and re-layouts: 5.96 us -> 4.51 us
where the time goes in v2:
time: 60.8 us; the launch traced here: 60.4 us
  Pallas kernels  55.3 us (91%)
  local copies, waits for them, and re-layouts  4.51 us (7%)
  between operations  0.64 us (1%)
    pallas_call x1, Pallas kernels, fused(): pl.pallas_call(functools.partial(fused_kernel, n_tgt, n_cand, parts), out...  55.3 us
    unnamed x3, local copies, waits for them, and re-layouts  4.51 us

profile of v2, /device:TPU:0, one launch (start us, length us, event | category | flops | bytes accessed | tf_op | source)
XLA Modules:
  0.0 60.4 jit_solution(8529959183725680864)
XLA Ops:
  0.6 1.4 %copy.6.weight_ref = f32[32,16]{1,0:T(8,128)} copy(f32[32,16]{0,1:T(8,128)} %param.7) | data formatting | bytes 4096 | tf_op args[3]
  2.0 55.3 %shard_map.59 = (f32[32,1024]{1,0:T(8,128)}, f32[32,1024]{1,0:T(8,128)}) custom-call(bf16[1024,1024]{1,0:T(8,128)(2,1)} %cand_hbm.1, bf16[1024,1024]{1,0:T(8,128)(2,1)} %tgt_hbm.1, s32[1,2048]{1,0:T(1,128)} %bitcast.1, f32[32,16]{1,0:T(8,128)} %copy.6.weight_ref), custom_call_target="tpu_custom_call" | custom-call | tf_op jit(solution)/shard_map/pallas_call | solution.py:263
  57.3 1.6 %copy.9 = f32[32,1024]{1,0:T(8,128)} copy(f32[32,1024]{1,0:T(8,128)} %get-tuple-element.4) | data formatting | bytes 262144
  58.9 1.6 %copy.10 = f32[32,1024]{1,0:T(8,128)} copy(f32[32,1024]{1,0:T(8,128)} %get-tuple-element.5) | data formatting | bytes 262144

commit v3 on v2

--- a/solution.py
+++ b/solution.py
@@ -18,13 +18,14 @@
 F32 = jnp.float32
 BF16 = jnp.bfloat16
 NT_DIMS = (((1,), (1,)), ((), ()))
+TN_DIMS = (((0,), (0,)), ((), ()))
 NN_DIMS = (((1,), (0,)), ((), ()))
 
 
 def unit_rows(embedding):
     values = embedding.astype(jnp.float32)
     mean_sq = jnp.mean(values * values, axis=1, keepdims=True)
-    return (values * lax.rsqrt(mean_sq + 1e-06) * (1.0 / math.sqrt(values.shape[1]))).astype(
+    return (values * (lax.rsqrt(mean_sq + 1e-06) * (1.0 / math.sqrt(values.shape[1])))).astype(
         jnp.bfloat16
     )
 
@@ -48,13 +49,14 @@
     n_tgt, n_cand, parts, cand_hbm, tgt_hbm, member_ref, weight_ref, out_cand, out_tgt,
     cand_rows, tgt_rows, tgt_unit, raised, k_one, k_two, mass, cand_sums,
     row_slots, col_slots, task_slots, cand_slots, rs_send, rs_slots, ag_slots,
-    load_sems, x_send, x_recv, z_send, z_recv,
+    load_sems, x_send, x_recv, z_send, z_recv, rs_out, rs_in, ag_out, ag_in,
 ):
     xi, zi = lax.axis_index("tgt"), lax.axis_index("cand")
     rows, width = cand_hbm.shape
     cols = tgt_hbm.shape[0]
-    mixes, tasks = weight_ref.shape
-    share = cols // n_cand
+    tasks, mixes = weight_ref.shape
+    owners = (n_cand // 2 - 1, n_cand // 2)
+    share = cols // len(owners)
     group = mixes // parts
     tgt_total, cand_total = cols * n_tgt, rows * n_cand
     block = 256
@@ -118,15 +120,11 @@
         for copy in copies:
             copy.wait_recv()
 
-    def z_columns(d):
-        at = lax.rem(zi - d + n_cand, n_cand) * share
-        return pl.ds(pl.multiple_of(at, share), share)
-
     all_ids = lax.broadcasted_iota(jnp.int32, (tasks, tgt_total), 0)
     all_hot = (member_ref[...] == all_ids).astype(F32)
     weights = weight_ref[...]
     per_target = lax.dot_general(
-        weights, all_hot, NN_DIMS, precision=lax.Precision.HIGHEST, preferred_element_type=F32
+        weights, all_hot, TN_DIMS, precision=lax.Precision.HIGHEST, preferred_element_type=F32
     )
     ratio = float(cand_total) / jnp.sum(per_target, axis=1, keepdims=True)
     own = pl.ds(pl.multiple_of(xi * cols, cols), cols)
@@ -135,7 +133,7 @@
     ).astype(F32)
     mass[...] = (
         lax.dot_general(
-            weights, own_hot, NN_DIMS, precision=lax.Precision.HIGHEST, preferred_element_type=F32
+            weights, own_hot, TN_DIMS, precision=lax.Precision.HIGHEST, preferred_element_type=F32
         )
         * ratio
     )
@@ -144,13 +142,17 @@
         copy.wait()
         at = pl.ds(index * block, block)
         tgt_unit[at, :] = unit_rows(tgt_rows[at, :])
-    for index, copy in enumerate(cand_loads):
+    for copy in cand_loads:
         copy.wait()
-        at = pl.ds(index * block, block)
+    ones = jnp.ones((16, cols), BF16)
+    for first in range(0, rows, block):
+        at = pl.ds(first, block)
         scores = contract_last(unit_rows(cand_rows[at, :]), tgt_unit[...])
         power = jnp.exp(scores * (1.0 / EPS_FIRST))
         raised[at, :] = power
-        k_one[at, :] = (power * (1.0 / tgt_total)).astype(BF16)
+        kernel_rows = (power * (1.0 / tgt_total)).astype(BF16)
+        k_one[at, :] = kernel_rows
+        row_slots[0, :, at] = contract_last(ones, kernel_rows)[:1]
 
     def square(first, last):
         def step(b, carry):
@@ -163,8 +165,6 @@
 
     pl.semaphore_wait(barrier, n_tgt - 1 + n_cand - 1)
 
-    ones = jnp.ones((16, cols), BF16)
-    row_slots[0] = contract_last(ones, k_one[...])[:1]
     copies = x_start(row_slots, 0)
     square(0, rows // 2)
     arrive(copies)
@@ -182,44 +182,94 @@
     task_slots[0] = join_rows(contract_last(split_rows(own_hot / col_sum), k_one[...]))
     arrive(x_start(task_slots, 1))
     cand_sums[...] = ratio * lax.dot_general(
-        weights, x_sum(task_slots), NN_DIMS, precision=lax.Precision.HIGHEST,
+        weights, x_sum(task_slots), TN_DIMS, precision=lax.Precision.HIGHEST,
         preferred_element_type=F32,
     )
 
     def of(part):
         return pl.ds(part * group, group)
 
+    def half(o):
+        return pl.ds(o * share, share)
+
+    def to_owner(turn, part, o):
+        return pltpu.make_async_remote_copy(
+            src_ref=rs_send.at[turn, part, o], dst_ref=rs_slots.at[turn, part, zi],
+            send_sem=rs_out.at[turn, part, o], recv_sem=rs_in.at[turn, part, zi],
+            device_id={"cand": owners[o]}, device_id_type=MESH,
+        )
+
+    def from_owner(turn, part, o, peer):
+        return pltpu.make_async_remote_copy(
+            src_ref=ag_slots.at[turn, part, o], dst_ref=ag_slots.at[turn, part, o],
+            send_sem=ag_out.at[turn, part, peer], recv_sem=ag_in.at[turn, part, o],
+            device_id={"cand": peer}, device_id_type=MESH,
+        )
+
+    def owned_from(turn, part, o, source):
+        return pltpu.make_async_remote_copy(
+            src_ref=rs_send.at[turn, part, o], dst_ref=rs_slots.at[turn, part, source],
+            send_sem=rs_out.at[turn, part, o], recv_sem=rs_in.at[turn, part, source],
+            device_id={"cand": source}, device_id_type=MESH,
+        )
+
+    def others(o):
+        return [z for z in range(n_cand) if z != owners[o]]
+
+    halves = range(len(owners))
+
     def tgt_send(kernel, turn, part):
         lhs = split_rows(1.0 / cand_sums[of(part), :])
-
-        def columns(peer):
-            at = pl.ds(pl.multiple_of(peer * share, share), share)
-            return join_rows(
-                lax.dot_general(lhs, kernel[:, at], NN_DIMS, preferred_element_type=F32)
+        for o in halves:
+            value = join_rows(
+                lax.dot_general(lhs, kernel[:, half(o)], NN_DIMS, preferred_element_type=F32)
             )
-
-        out, slots = rs_send.at[turn, part], rs_slots.at[turn, part]
-        copies = []
-        for d in range(1, n_cand):
-            out[d - 1] = columns(lax.rem(zi + d, n_cand))
-            copies.append(
-                send(out.at[d - 1], slots.at[d], zs, 1 + turn * parts + part, d, z_peer(d))
-            )
-        slots[0] = columns(zi)
-        return copies
-
-    def tgt_finish(copies, turn, part, change):
-        arrive(copies)
-        slots = ag_slots.at[turn, part]
-        slots[0] = change(mass[of(part), z_columns(0)] / z_sum(rs_slots.at[turn, part]))
-        return z_start(slots, 1 + (1 + ITERS + turn) * parts + part)
-
-    def cand_send(copies, turn, part):
+            rs_send[turn, part, o] = value
+
+            @pl.when(zi != owners[o])
+            def _():
+                to_owner(turn, part, o).start()
+
+    def tgt_finish(turn, part, change):
+        for o in halves:
+
+            @pl.when(zi == owners[o])
+            def _():
+                for z in others(o):
+                    owned_from(turn, part, o, z).wait_recv()
+                total = None
+                for z in range(n_cand):
+                    own = z == owners[o]
+                    value = rs_send[turn, part, o] if own else rs_slots[turn, part, z]
+                    total = value if total is None else total + value
+                ag_slots[turn, part, o] = change(mass[of(part), half(o)] / total)
+                for z in others(o):
+                    from_owner(turn, part, o, z).start()
+
+    def gathered(turn, part):
+        for o in halves:
+
+            @pl.when(zi != owners[o])
+            def _():
+                from_owner(turn, part, o, owners[o]).wait_recv()
+
+    def drain(turn, part):
+        for o in halves:
+
+            @pl.when(zi != owners[o])
+            def _():
+                to_owner(turn, part, o).wait_send()
+
+            @pl.when(zi == owners[o])
+            def _():
+                for z in others(o):
+                    from_owner(turn, part, o, z).wait_send()
+
+    def cand_send(turn, part):
+        gathered(turn, part)
         total = None
-        for d in range(n_cand):
-            if d:
-                copies[d - 1].wait_recv()
-            value = contract_last(split_rows(ag_slots[turn, part, d]), k_two[:, z_columns(d)])
+        for o in halves:
+            value = contract_last(split_rows(ag_slots[turn, part, o]), k_two[:, half(o)])
             total = value if total is None else total + value
         cand_slots[turn, part, 0] = join_rows(total)
         return x_start(cand_slots.at[turn, part], 2 + turn * parts + part)
@@ -232,22 +282,26 @@
         return scale
 
     each = range(parts)
-    reduced = [tgt_send(k_one, 0, part) for part in each]
+    for part in each:
+        tgt_send(k_one, 0, part)
     changes = (jnp.square,) + (keep,) * (ITERS - 1)
     for turn in range(ITERS):
-        gathered = [tgt_finish(reduced[part], turn, part, changes[turn]) for part in each]
-        summed = [cand_send(gathered[part], turn, part) for part in each]
-        reduced = []
+        for part in each:
+            tgt_finish(turn, part, changes[turn])
+        summed = [cand_send(turn, part) for part in each]
         for part in each:
             cand_finish(summed[part], turn, part)
-            reduced.append(tgt_send(k_two, 1 + turn, part))
+            tgt_send(k_two, 1 + turn, part)
     out_cand[...] = -jnp.log(cand_sums[...])
-    gathered = [tgt_finish(reduced[part], ITERS, part, jnp.log) for part in each]
     for part in each:
-        for d in range(n_cand):
-            if d:
-                gathered[part][d - 1].wait_recv()
-            out_tgt[of(part), z_columns(d)] = ag_slots[ITERS, part, d]
+        tgt_finish(ITERS, part, jnp.log)
+    for part in each:
+        gathered(ITERS, part)
+        for o in halves:
+            out_tgt[of(part), half(o)] = ag_slots[ITERS, part, o]
+    for turn in range(1 + ITERS):
+        for part in each:
+            drain(turn, part)
     for copy in pending:
         copy.wait_send()
 
@@ -257,7 +311,7 @@
     rows, width = candidates.shape
     cols = targets.shape[0]
     mixes, tasks = mix_weight.shape
-    share = cols // n_cand
+    share = cols // 2
     parts = 2 if mixes % 16 == 0 else 1
     group = mixes // parts
     return tuple(pl.pallas_call(
@@ -282,19 +336,23 @@
             pltpu.VMEM((n_cand, 1, cols), F32),
             pltpu.VMEM((n_tgt, tasks, rows), F32),
             pltpu.VMEM((ITERS, parts, n_tgt, group, rows), F32),
-            pltpu.VMEM((1 + ITERS, parts, n_cand - 1, group, share), F32),
+            pltpu.VMEM((1 + ITERS, parts, 2, group, share), F32),
             pltpu.VMEM((1 + ITERS, parts, n_cand, group, share), F32),
-            pltpu.VMEM((1 + ITERS, parts, n_cand, group, share), F32),
+            pltpu.VMEM((1 + ITERS, parts, 2, group, share), F32),
             pltpu.SemaphoreType.DMA((2, max(rows, cols) // 256)),
             pltpu.SemaphoreType.DMA((2 + ITERS * parts, n_tgt - 1)),
             pltpu.SemaphoreType.DMA((2 + ITERS * parts, n_tgt - 1)),
-            pltpu.SemaphoreType.DMA((1 + 2 * (1 + ITERS) * parts, n_cand - 1)),
-            pltpu.SemaphoreType.DMA((1 + 2 * (1 + ITERS) * parts, n_cand - 1)),
+            pltpu.SemaphoreType.DMA((1, n_cand - 1)),
+            pltpu.SemaphoreType.DMA((1, n_cand - 1)),
+            pltpu.SemaphoreType.DMA((1 + ITERS, parts, 2)),
+            pltpu.SemaphoreType.DMA((1 + ITERS, parts, n_cand)),
+            pltpu.SemaphoreType.DMA((1 + ITERS, parts, n_cand)),
+            pltpu.SemaphoreType.DMA((1 + ITERS, parts, 2)),
         ],
         compiler_params=pltpu.CompilerParams(
             collective_id=0, has_side_effects=True, vmem_limit_bytes=56 * 1024 * 1024
         ),
-    )(candidates, targets, member.reshape(1, -1), mix_weight))
+    )(candidates, targets, member.reshape(1, -1), mix_weight.T))
 
 
 def target_mass(own_member, member, mix_weight, cand_total):
@@ -348,7 +406,7 @@
     n_tgt, n_cand = mesh.shape["tgt"], mesh.shape["cand"]
 
     def local(candidates, targets, member, mix_weight):
-        lanes = targets.shape[0] % (128 * n_cand) == 0
+        lanes = targets.shape[0] % (128 * n_cand) == 0 and candidates.shape[0] % 256 == 0
         step = fused if lanes and n_cand > 1 and n_tgt > 1 else by_collectives
         return step(candidates, targets, member, mix_weight)
 

time: 60.8 us -> 57 us (0.938)
  Pallas kernels: 55.3 us -> 53 us
  local copies, waits for them, and re-layouts: 4.51 us -> 3.14 us
    pallas_call x1, Pallas kernels: 55.3 us -> 53 us  [fused(): pl.pallas_call(functools.partial(fused_kernel, n_tgt, n_cand, parts), out...]
    unnamed x3 -> x2, local copies, waits for them, and re-layouts: 4.51 us -> 3.14 us
where the time goes in v3:
time: 57 us; the launch traced here: 56.8 us
  Pallas kernels  53 us (93%)
  local copies, waits for them, and re-layouts  3.14 us (6%)
  between operations  0.64 us (1%)
    pallas_call x1, Pallas kernels, fused(): pl.pallas_call(functools.partial(fused_kernel, n_tgt, n_cand, parts), out...  53 us
    unnamed x2, local copies, waits for them, and re-layouts  3.14 us

profile of v3, /device:TPU:0, one launch (start us, length us, event | category | flops | bytes accessed | tf_op | source)
XLA Modules:
  0.0 56.8 jit_solution(4462253077082502905)
XLA Ops:
  0.6 53.0 %shard_map.59 = (f32[32,1024]{1,0:T(8,128)}, f32[32,1024]{1,0:T(8,128)}) custom-call(bf16[1024,1024]{1,0:T(8,128)(2,1)} %cand_hbm.1, bf16[1024,1024]{1,0:T(8,128)(2,1)} %tgt_hbm.1, s32[1,2048]{1,0:T(1,128)} %bitcast.2, f32[16,32]{1,0:T(8,128)} %bitcast.3), custom_call_target="tpu_custom_call" | custom-call | tf_op jit(solution)/shard_map/pallas_call | solution.py:317
  53.6 1.6 %copy.8 = f32[32,1024]{1,0:T(8,128)} copy(f32[32,1024]{1,0:T(8,128)} %get-tuple-element.4) | data formatting | bytes 262144
  55.2 1.6 %copy.9 = f32[32,1024]{1,0:T(8,128)} copy(f32[32,1024]{1,0:T(8,128)} %get-tuple-element.5) | data formatting | bytes 262144

commit v4 on v3

--- a/solution.py
+++ b/solution.py
@@ -46,12 +46,12 @@
 
 
 def fused_kernel(
-    n_tgt, n_cand, parts, cand_hbm, tgt_hbm, member_ref, weight_ref, out_cand, out_tgt,
+    n_tgt, n_cand, n_mix, parts, cand_hbm, tgt_hbm, member_ref, weight_ref, out_cand, out_tgt,
     cand_rows, tgt_rows, tgt_unit, raised, k_one, k_two, mass, cand_sums,
-    row_slots, col_slots, task_slots, cand_slots, rs_send, rs_slots, ag_slots,
-    load_sems, x_send, x_recv, z_send, z_recv, rs_out, rs_in, ag_out, ag_in,
+    row_part, row_slots, col_slots, task_slots, cand_slots, rs_send, rs_slots, ag_slots,
+    load_sems, x_send, x_recv, z_send, z_recv, row_out, row_in, rs_out, rs_in, ag_out, ag_in,
 ):
-    xi, zi = lax.axis_index("tgt"), lax.axis_index("cand")
+    xi, zi, ci = lax.axis_index("tgt"), lax.axis_index("cand"), lax.axis_index("mix")
     rows, width = cand_hbm.shape
     cols = tgt_hbm.shape[0]
     tasks, mixes = weight_ref.shape
@@ -76,12 +76,16 @@
     def x_peer(d):
         return {"tgt": lax.rem(xi + d, n_tgt)}
 
+    def xc_peer(d, e):
+        return {"tgt": lax.rem(xi + d, n_tgt), "mix": lax.rem(ci + e, n_mix)}
+
     def z_peer(d):
         return {"cand": lax.rem(zi + d, n_cand)}
 
     barrier = pltpu.get_barrier_semaphore()
     for d in range(1, n_tgt):
-        pl.semaphore_signal(barrier, inc=1, device_id=x_peer(d), device_id_type=MESH)
+        for e in range(n_mix):
+            pl.semaphore_signal(barrier, inc=1, device_id=xc_peer(d, e), device_id_type=MESH)
     for d in range(1, n_cand):
         pl.semaphore_signal(barrier, inc=1, device_id=z_peer(d), device_id_type=MESH)
 
@@ -145,14 +149,33 @@
     for copy in cand_loads:
         copy.wait()
     ones = jnp.ones((16, cols), BF16)
-    for first in range(0, rows, block):
-        at = pl.ds(first, block)
+    early = rows // n_mix
+
+    def build(first):
+        at = pl.ds(pl.multiple_of(first, block), block)
         scores = contract_last(unit_rows(cand_rows[at, :]), tgt_unit[...])
         power = jnp.exp(scores * (1.0 / EPS_FIRST))
         raised[at, :] = power
         kernel_rows = (power * (1.0 / tgt_total)).astype(BF16)
         k_one[at, :] = kernel_rows
-        row_slots[0, :, at] = contract_last(ones, kernel_rows)[:1]
+        return contract_last(ones, kernel_rows)[:1]
+
+    for first in range(0, early, block):
+        row_part[ci, :, pl.ds(first, block)] = build(ci * early + first)
+    pl.semaphore_wait(barrier, (n_tgt - 1) * n_mix + n_cand - 1)
+    row_copies = []
+    for d in range(1, n_tgt):
+        for e in range(n_mix):
+            row_copies.append(pltpu.make_async_remote_copy(
+                src_ref=row_part.at[ci], dst_ref=row_slots.at[d, ci],
+                send_sem=row_out.at[d - 1, e], recv_sem=row_in.at[d - 1, ci],
+                device_id=xc_peer(d, e), device_id_type=MESH,
+            ))
+            row_copies[-1].start()
+    for later in range(1, n_mix):
+        other = lax.rem(ci + later, n_mix)
+        for first in range(0, early, block):
+            row_part[other, :, pl.ds(first, block)] = build(other * early + first)
 
     def square(first, last):
         def step(b, carry):
@@ -163,12 +186,22 @@
 
         lax.fori_loop(first // 64, last // 64, step, 0)
 
-    pl.semaphore_wait(barrier, n_tgt - 1 + n_cand - 1)
-
-    copies = x_start(row_slots, 0)
+
     square(0, rows // 2)
-    arrive(copies)
-    scale_row = 1.0 / x_sum(row_slots)
+    for d in range(1, n_tgt):
+        for e in range(n_mix):
+            pltpu.make_async_remote_copy(
+                src_ref=row_part.at[e], dst_ref=row_slots.at[d, e],
+                send_sem=row_out.at[d - 1, e], recv_sem=row_in.at[d - 1, e],
+                device_id=x_peer(d), device_id_type=MESH,
+            ).wait_recv()
+    row_sums = []
+    for e in range(n_mix):
+        value = row_part[e]
+        for d in range(1, n_tgt):
+            value = value + row_slots[d, e]
+        row_sums.append(value)
+    scale_row = 1.0 / jnp.concatenate(row_sums, axis=1)
     place = lax.broadcasted_iota(jnp.int32, (16, rows), 0)
     head = scale_row.astype(BF16).astype(F32)
     lhs = jnp.where(place == 0, head, jnp.where(place == 1, scale_row - head, 0.0)).astype(BF16)
@@ -302,7 +335,7 @@
     for turn in range(1 + ITERS):
         for part in each:
             drain(turn, part)
-    for copy in pending:
+    for copy in pending + row_copies:
         copy.wait_send()
 
 
@@ -311,11 +344,12 @@
     rows, width = candidates.shape
     cols = targets.shape[0]
     mixes, tasks = mix_weight.shape
+    n_mix = lax.axis_size("mix")
     share = cols // 2
     parts = 2 if mixes % 16 == 0 else 1
     group = mixes // parts
     return tuple(pl.pallas_call(
-        functools.partial(fused_kernel, n_tgt, n_cand, parts),
+        functools.partial(fused_kernel, n_tgt, n_cand, n_mix, parts),
         out_shape=(
             jax.ShapeDtypeStruct((mixes, rows), F32),
             jax.ShapeDtypeStruct((mixes, cols), F32),
@@ -332,7 +366,8 @@
             pltpu.VMEM((rows, cols), BF16),
             pltpu.VMEM((mixes, cols), F32),
             pltpu.VMEM((mixes, rows), F32),
-            pltpu.VMEM((n_tgt, 1, rows), F32),
+            pltpu.VMEM((n_mix, 1, rows // n_mix), F32),
+            pltpu.VMEM((n_tgt, n_mix, 1, rows // n_mix), F32),
             pltpu.VMEM((n_cand, 1, cols), F32),
             pltpu.VMEM((n_tgt, tasks, rows), F32),
             pltpu.VMEM((ITERS, parts, n_tgt, group, rows), F32),
@@ -344,6 +379,8 @@
             pltpu.SemaphoreType.DMA((2 + ITERS * parts, n_tgt - 1)),
             pltpu.SemaphoreType.DMA((1, n_cand - 1)),
             pltpu.SemaphoreType.DMA((1, n_cand - 1)),
+            pltpu.SemaphoreType.DMA((n_tgt - 1, n_mix)),
+            pltpu.SemaphoreType.DMA((n_tgt - 1, n_mix)),
             pltpu.SemaphoreType.DMA((1 + ITERS, parts, 2)),
             pltpu.SemaphoreType.DMA((1 + ITERS, parts, n_cand)),
             pltpu.SemaphoreType.DMA((1 + ITERS, parts, n_cand)),
@@ -406,7 +443,7 @@
     n_tgt, n_cand = mesh.shape["tgt"], mesh.shape["cand"]
 
     def local(candidates, targets, member, mix_weight):
-        lanes = targets.shape[0] % (128 * n_cand) == 0 and candidates.shape[0] % 256 == 0
+        lanes = targets.shape[0] % (128 * n_cand) == 0 and candidates.shape[0] % 512 == 0
         step = fused if lanes and n_cand > 1 and n_tgt > 1 else by_collectives
         return step(candidates, targets, member, mix_weight)
 

time: 57 us -> 55.8 us (0.979)
  Pallas kernels: 53 us -> 51.7 us
    pallas_call x1, Pallas kernels: 53 us -> 51.7 us  [fused(): pl.pallas_call(functools.partial(fused_kernel, n_tgt, n_cand, n_mix, part...]
where the time goes in v4:
time: 55.8 us; the launch traced here: 55.5 us
  Pallas kernels  51.7 us (93%)
  local copies, waits for them, and re-layouts  3.14 us (6%)
  between operations  0.64 us (1%)
    pallas_call x1, Pallas kernels, fused(): pl.pallas_call(functools.partial(fused_kernel, n_tgt, n_cand, n_mix, part...  51.7 us
    unnamed x2, local copies, waits for them, and re-layouts  3.14 us

profile of v4, /device:TPU:0, one launch (start us, length us, event | category | flops | bytes accessed | tf_op | source)
XLA Modules:
  0.0 55.5 jit_solution(424511644947086374)
XLA Ops:
  0.6 51.7 %shard_map.59 = (f32[32,1024]{1,0:T(8,128)}, f32[32,1024]{1,0:T(8,128)}) custom-call(bf16[1024,1024]{1,0:T(8,128)(2,1)} %cand_hbm.1, bf16[1024,1024]{1,0:T(8,128)(2,1)} %tgt_hbm.1, s32[1,2048]{1,0:T(1,128)} %bitcast.2, f32[16,32]{1,0:T(8,128)} %bitcast.3), custom_call_target="tpu_custom_call" | custom-call | tf_op jit(solution)/shard_map/pallas_call | solution.py:351
  52.4 1.6 %copy.8 = f32[32,1024]{1,0:T(8,128)} copy(f32[32,1024]{1,0:T(8,128)} %get-tuple-element.4) | data formatting | bytes 262144
  53.9 1.6 %copy.9 = f32[32,1024]{1,0:T(8,128)} copy(f32[32,1024]{1,0:T(8,128)} %get-tuple-element.5) | data formatting | bytes 262144

commit v5 on v4

--- a/solution.py
+++ b/solution.py
@@ -187,7 +187,6 @@
         lax.fori_loop(first // 64, last // 64, step, 0)
 
 
-    square(0, rows // 2)
     for d in range(1, n_tgt):
         for e in range(n_mix):
             pltpu.make_async_remote_copy(
@@ -208,7 +207,7 @@
     part = lax.dot_general(lhs, k_one[...], NN_DIMS, preferred_element_type=F32)
     col_slots[0] = part[:1] + part[1:2]
     copies = z_start(col_slots, 0)
-    square(rows // 2, rows)
+    square(0, rows)
     arrive(copies)
     col_sum = z_sum(col_slots)
 
@@ -223,13 +222,16 @@
         return pl.ds(part * group, group)
 
     def half(o):
-        return pl.ds(o * share, share)
+        return pl.ds(o * share if isinstance(o, int) else pl.multiple_of(o * share, share), share)
+
+    far = 1 - zi // owners[1]
+    near = 1 - far
 
     def to_owner(turn, part, o):
         return pltpu.make_async_remote_copy(
             src_ref=rs_send.at[turn, part, o], dst_ref=rs_slots.at[turn, part, zi],
             send_sem=rs_out.at[turn, part, o], recv_sem=rs_in.at[turn, part, zi],
-            device_id={"cand": owners[o]}, device_id_type=MESH,
+            device_id={"cand": owners[0] + o}, device_id_type=MESH,
         )
 
     def from_owner(turn, part, o, peer):
@@ -253,13 +255,15 @@
 
     def tgt_send(kernel, turn, part):
         lhs = split_rows(1.0 / cand_sums[of(part), :])
-        for o in halves:
-            value = join_rows(
+        for o in (far, near):
+            rs_send[turn, part, o] = join_rows(
                 lax.dot_general(lhs, kernel[:, half(o)], NN_DIMS, preferred_element_type=F32)
             )
-            rs_send[turn, part, o] = value
-
-            @pl.when(zi != owners[o])
+            if o is far:
+                to_owner(turn, part, o).start()
+                continue
+
+            @pl.when(zi != owners[0] + o)
             def _():
                 to_owner(turn, part, o).start()
 
@@ -279,12 +283,10 @@
                 for z in others(o):
                     from_owner(turn, part, o, z).start()
 
-    def gathered(turn, part):
-        for o in halves:
-
-            @pl.when(zi != owners[o])
-            def _():
-                from_owner(turn, part, o, owners[o]).wait_recv()
+    def gathered(turn, part, o):
+        @pl.when(zi != owners[0] + o)
+        def _():
+            from_owner(turn, part, o, owners[0] + o).wait_recv()
 
     def drain(turn, part):
         for o in halves:
@@ -299,9 +301,9 @@
                     from_owner(turn, part, o, z).wait_send()
 
     def cand_send(turn, part):
-        gathered(turn, part)
         total = None
-        for o in halves:
+        for o in (near, far):
+            gathered(turn, part, o)
             value = contract_last(split_rows(ag_slots[turn, part, o]), k_two[:, half(o)])
             total = value if total is None else total + value
         cand_slots[turn, part, 0] = join_rows(total)
@@ -329,8 +331,8 @@
     for part in each:
         tgt_finish(ITERS, part, jnp.log)
     for part in each:
-        gathered(ITERS, part)
         for o in halves:
+            gathered(ITERS, part, o)
             out_tgt[of(part), half(o)] = ag_slots[ITERS, part, o]
     for turn in range(1 + ITERS):
         for part in each:
@@ -444,7 +446,7 @@
 
     def local(candidates, targets, member, mix_weight):
         lanes = targets.shape[0] % (128 * n_cand) == 0 and candidates.shape[0] % 512 == 0
-        step = fused if lanes and n_cand > 1 and n_tgt > 1 else by_collectives
+        step = fused if lanes and n_cand % 2 == 0 and n_tgt > 1 else by_collectives
         return step(candidates, targets, member, mix_weight)
 
     return jax.shard_map(local, mesh=mesh, in_specs=in_specs, out_specs=out_specs, check_vma=False)

time: 55.8 us -> 54.6 us (0.978)
  Pallas kernels: 51.7 us -> 50.5 us
    pallas_call x1, Pallas kernels: 51.7 us -> 50.5 us  [fused(): pl.pallas_call(functools.partial(fused_kernel, n_tgt, n_cand, n_mix, part...]
where the time goes in v5:
time: 54.6 us; the launch traced here: 54.3 us
  Pallas kernels  50.5 us (92%)
  local copies, waits for them, and re-layouts  3.14 us (6%)
  between operations  0.64 us (1%)
    pallas_call x1, Pallas kernels, fused(): pl.pallas_call(functools.partial(fused_kernel, n_tgt, n_cand, n_mix, part...  50.5 us
    unnamed x2, local copies, waits for them, and re-layouts  3.14 us

profile of v5, /device:TPU:0, one launch (start us, length us, event | category | flops | bytes accessed | tf_op | source)
XLA Modules:
  0.0 54.3 jit_solution(17373488122455864470)
XLA Ops:
  0.6 50.5 %shard_map.59 = (f32[32,1024]{1,0:T(8,128)}, f32[32,1024]{1,0:T(8,128)}) custom-call(bf16[1024,1024]{1,0:T(8,128)(2,1)} %cand_hbm.1, bf16[1024,1024]{1,0:T(8,128)(2,1)} %tgt_hbm.1, s32[1,2048]{1,0:T(1,128)} %bitcast.2, f32[16,32]{1,0:T(8,128)} %bitcast.3), custom_call_target="tpu_custom_call" | custom-call | tf_op jit(solution)/shard_map/pallas_call | solution.py:353
  51.2 1.6 %copy.8 = f32[32,1024]{1,0:T(8,128)} copy(f32[32,1024]{1,0:T(8,128)} %get-tuple-element.4) | data formatting | bytes 262144
  52.7 1.6 %copy.9 = f32[32,1024]{1,0:T(8,128)} copy(f32[32,1024]{1,0:T(8,128)} %get-tuple-element.5) | data formatting | bytes 262144
